TPU v7x, 32 devices: a whole 2x2x4 slice. The times are simulated.
32 devices in a mesh: sp: 16 (over z, y, x), pb: 2 (over core).
Axes of the slice: x: 2, y: 2, z: 4, core: 2. Of those that a mesh axis runs over, the one named last changes fastest.
Arguments:
- amplitudes: bfloat16 [40, 1024, 1024], P('pb', 'sp'), may hold values from -6 to 6
- virtuals: bfloat16 [1400, 1024], replicated, may hold values from -0.375 to 0.375
- energies: float32 [1024], replicated, may hold values from 0.02 to 0.2
- integrals: bfloat16 [2048, 2048], P('sp'), may hold values from -0.125 to 0.125
- screened: int32 [16, 16], P('sp'), may hold values from 0 to 15, as said below
- counts: int32 [16], P('sp'), may hold values from 1 to 16, 128 in all
- offsets: int32 [2, 16], replicated, may hold values from 0 to 1384
- coupling: bfloat16 [40, 40], P('pb'), may hold values from -1 to 1
Outputs:
- residual: bfloat16 [40, 1024, 1024], P('pb', 'sp')
Inputs may be any that keep to these rules, and one draw needn't show every extreme that they name: `screened`: each row names 16 different blocks.
All inputs are finite; a program needn't handle non-finite values. No bound on the sum of `counts` on one device may be relied on, other than what follows from the above.
Results may differ from a plain program's by a relative error of at most 0.01.
Values may be sent and summed in bfloat16 or wider, within the bound.
No kernel may reach another device: no remote copies, remote signals or barrier semaphores. Data moves between devices by JAX's collectives and lax.ppermute only.
A program may use at most 64 MiB of HBM per device.

v0:
```python
import jax
import jax.numpy as jnp
from jax import lax
from jax.sharding import PartitionSpec as P

SHELL_ROW = 8
SHELL_COL = 16


def shards(amplitudes, virtuals, energies, integrals, screened, counts, offsets, coupling):
    pairs = amplitudes.shape[0]
    ext_rows = amplitudes.shape[1]
    width = SHELL_ROW * SHELL_COL
    nblk = lax.axis_size("sp")
    first = lax.axis_index("sp") * ext_rows
    local_cols = lax.dynamic_slice_in_dim(virtuals, first, ext_rows, 1)
    half = jnp.einsum(
        "pab,nb->pan", amplitudes, virtuals, preferred_element_type=jnp.float32
    ).astype(jnp.bfloat16)
    row_span = jnp.arange(SHELL_ROW, dtype=jnp.int32)
    col_span = jnp.arange(SHELL_COL, dtype=jnp.int32)
    lows = offsets[0]
    highs = offsets[1]
    left = local_cols[lows[:, None] + row_span[None, :]]
    right = half[:, :, highs[:, None] + col_span[None, :]]
    term = jnp.einsum("bia,pabs->bpis", left, right, preferred_element_type=jnp.float32)
    ao_all = lax.psum(term.reshape(nblk, pairs, width), "sp").astype(jnp.bfloat16)
    slots = screened.shape[1]
    live = (jnp.arange(slots, dtype=jnp.int32) < counts[0]).astype(jnp.bfloat16)
    chosen = jnp.take(ao_all, screened[0], axis=0) * live[:, None, None]
    slab = integrals.reshape(width, slots, width)
    raw = jnp.einsum("rkc,kpc->pr", slab, chosen, preferred_element_type=jnp.float32).astype(
        jnp.bfloat16
    )
    every = lax.all_gather(raw[None], ("sp", "pb"), axis=0, tiled=True)
    every = every.reshape(nblk, coupling.shape[1], width)
    k_all = jnp.einsum("pq,bqc->bpc", coupling, every, preferred_element_type=jnp.float32).astype(
        jnp.bfloat16
    )
    left_all = local_cols[offsets[0][:, None] + row_span[None, :]]
    right_rows = virtuals[offsets[1][:, None] + col_span[None, :]]
    square = k_all.reshape(nblk, pairs, SHELL_ROW, SHELL_COL)
    upper = jnp.einsum(
        "bia,bpis->pabs", left_all, square, preferred_element_type=jnp.float32
    ).astype(jnp.bfloat16)
    inner = jnp.einsum("pabs,bsn->pan", upper, right_rows, preferred_element_type=jnp.float32)
    own_energy = lax.dynamic_slice_in_dim(energies, first, ext_rows)
    diag = own_energy[:, None] + energies[None, :]
    return (inner + diag[None] * amplitudes.astype(jnp.float32)).astype(jnp.bfloat16)


def solution(mesh):
    return jax.shard_map(
        shards,
        mesh=mesh,
        in_specs=(
            P("pb", "sp", None),
            P(),
            P(),
            P("sp", None),
            P("sp", None),
            P("sp"),
            P(),
            P("pb", None),
        ),
        out_specs=P("pb", "sp", None),
        check_vma=False,
    )
```

profile of v0, /device:TPU:0, one launch (start us, length us, event | category | flops | bytes accessed | tf_op | source)
XLA Modules:
  0.0 168.3 jit_solution(11485403471382570395)
XLA Ops:
  0.0 1.8 %copy-done = bf16[1400,1024]{1,0:T(8,128)(2,1)S(1)} copy-done((bf16[1400,1024]{1,0:T(8,128)(2,1)S(1)}, bf16[1400,1024]{1,0:T(8,128)(2,1)}, u32[]{:S(2)}) %copy-start) | copy-done | bytes 2867224
  1.8 0.2 constant_dynamic-slice_fusion
  2.0 0.8 slice_bitcast_fusion
  2.7 0.1 compare_select_fusion
  2.8 0.1 reshape.178
  2.9 0.7 gather_fusion.1
  3.7 0.1 reshape.170
  3.8 7.6 %convolution_convert_fusion = bf16[20,64,1400]{2,1,0:T(8,128)(2,1)} fusion(bf16[20,64,1024]{2,1,0:T(8,128)(2,1)} %param.8, bf16[1400,1024]{1,0:T(8,128)(2,1)S(1)} %copy-done), kind=kOutput, calls=%fused_computation.6 | convolution fusion | flops 3671808000 | bytes 9072640 | tf_op jit(solution)/shard_map/pab,nb->pan/dot_general | solution.py:17
  11.4 10.8 %copy.25 = bf16[20,64,1400]{1,0,2:T(8,128)(2,1)} copy(bf16[20,64,1400]{2,1,0:T(8,128)(2,1)} %convolution_convert_fusion) | data formatting | bytes 7168000 | tf_op jit(solution)/shard_map/convert_element_type | solution.py:19
  22.2 5.5 %gather_fusion = bf16[256,20,64]{2,1,0:T(8,128)(2,1)} fusion(bf16[20,64,1400]{1,0,2:T(8,128)(2,1)} %copy.25, s32[1024]{0:T(1024)S(1)} %pad_clamp_fusion.2), kind=kCustom, calls=%fused_computation | custom fusion | bytes 1311744 | tf_op jit(solution)/shard_map/gather | solution.py:25
  27.6 5.1 %convolution_bitcast_fusion = f32[16,20,8,16]{1,2,3,0:T(8,128)} fusion(bf16[20,64,16,16]{1,0,3,2:T(8,128)(2,1)} %bitcast.75, bf16[128,64]{1,0:T(8,128)(2,1)S(1)} %gather_fusion.1), kind=kOutput, calls=%fused_computation.10 | convolution fusion | flops 5242880 | bytes 835584 | tf_op jit(solution)/shard_map/bia,pabs->bpis/dot_general | solution.py:26
  32.7 3.2 %copy.35 = f32[16,20,8,16]{3,2,1,0:T(8,128)} copy(f32[16,20,8,16]{1,2,3,0:T(8,128)} %convolution_bitcast_fusion) | data formatting | bytes 327680 | tf_op jit(solution)/shard_map/reshape | solution.py:27
  35.9 1.7 %reshape.214 = f32[16,20,128]{2,1,0:T(8,128)S(1)} reshape(f32[16,20,8,16]{3,2,1,0:T(8,128)} %copy.35) | data formatting | bytes 327680 | tf_op jit(solution)/shard_map/reshape | solution.py:27
  37.6 80.3 %all-reduce.1 = bf16[16,20,128]{2,1,0:T(8,128)(2,1)S(1)} all-reduce(f32[16,20,128]{2,1,0:T(8,128)S(1)} %reshape.214), channel_id=1, replica_groups=mesh['sp'=16,'pb'=2] {'sp'}, use_global_device_ids=true, to_apply=%region_0.0 | all-reduce | flops 40960 | bytes 245760 | tf_op jit(solution)/shard_map/psum | solution.py:27
  117.9 0.6 gather_fusion.2
  119.2 1.3 fusion.5
  120.5 36.9 %all-gather.1 = bf16[32,20,128]{2,1,0:T(8,128)(2,1)S(1)} all-gather(bf16[1,20,128]{2,1,0:T(8,128)(2,1)S(1)} %fusion.5), channel_id=2, replica_groups=mesh['sp'=16,'pb'=2] {'sp','pb'}, dimensions={0}, use_global_device_ids=true | all-gather | bytes 168960 | tf_op jit(solution)/shard_map/all_gather | solution.py:35
  157.4 0.2 fusion.3
  157.6 0.6 copy.31
  158.2 1.3 reshape.167
  159.6 0.8 dynamic_slice.7
  160.3 1.5 broadcast_add_fusion
  161.8 2.1 %gather_fusion.3 = bf16[256,1024]{1,0:T(8,128)(2,1)} fusion(bf16[1400,1024]{1,0:T(8,128)(2,1)S(1)} %copy-done, s32[1024]{0:T(1024)} %copy-done.1), kind=kCustom, calls=%fused_computation.3 | custom fusion | bytes 1049600 | tf_op jit(solution)/shard_map/gather | solution.py:41
  163.9 4.4 %fusion = bf16[20,64,1024]{2,1,0:T(8,128)(2,1)} fusion(bf16[20,64,1024]{2,1,0:T(8,128)(2,1)} %param.8, f32[64,1024]{1,0:T(8,128)} %broadcast_add_fusion, bf16[16,16,1024,1]{2,1,0,3:T(8,128)(2,1)} %bitcast.76, bf16[16,20,8,16]{3,2,0,1:T(8,128)(2,1)S(1)} %reshape.167, bf16[128,64]{1,0:T(8,128)(2,1)S(1)} %gather_fusion.1), kind=kOutput, calls=%fused_computation.5 | convolution fusion | flops 681902080 | bytes 6127616 | tf_op jit(solution)/shard_map/pabs,bsn->pan/dot_general | solution.py:46
  (14 shorter events, 0.2 us)
Async XLA Ops:
  0.0 1.8 %copy-start = (bf16[1400,1024]{1,0:T(8,128)(2,1)S(1)}, bf16[1400,1024]{1,0:T(8,128)(2,1)}, u32[]{:S(2)}) copy-start(bf16[1400,1024]{1,0:T(8,128)(2,1)} %param.9) | copy-start | bytes 8601604
  3.8 18.4 %copy-start.1 = (s32[1024]{0:T(1024)}, s32[1024]{0:T(1024)S(1)}, u32[]{:S(2)}) copy-start(s32[1024]{0:T(1024)S(1)} %pad_clamp_fusion.2) | copy-start | bytes 12292
  27.6 90.3 %copy-start.3 = (s32[1,16]{1,0:T(1,128)S(1)}, s32[1,16]{1,0:T(1,128)}, u32[]{:S(2)}) copy-start(s32[1,16]{1,0:T(1,128)} %param.12) | copy-start | bytes 196
  32.7 124.7 %copy-start.2 = (bf16[20,40]{1,0:T(8,128)(2,1)S(1)}, bf16[20,40]{1,0:T(8,128)(2,1)}, u32[]{:S(2)}) copy-start(bf16[20,40]{1,0:T(8,128)(2,1)} %param.15) | copy-start | bytes 4804
where the time goes:
time: 169 us; the launch traced here: 168 us
  blocking collectives  117 us (69%)
  local copies, waits for them, and re-layouts  30.2 us (18%)
  matrix products  18.6 us (11%)
    psum x1, blocking collectives, shards(): lax.psum(term.reshape(nblk, pairs, width), 'sp').astype(jnp.bfloat16)  80.3 us
    all_gather x1, blocking collectives, shards(): every = lax.all_gather(raw[None], ('sp', 'pb'), axis=0, tiled=True)  36.9 us
    convert_element_type x1, local copies, waits for them, and re-layouts, shards(): half = jnp.einsum('pab,nb->pan', amplitudes, virtuals, preferred_element_...  10.8 us
    dot_general x1, matrix products, shards(): jnp.einsum('pab,nb->pan', amplitudes, virtuals, preferred_element_type=jn...  7.57 us
    gather x1, local copies, waits for them, and re-layouts, shards(): right = half[:, :, highs[:, None] + col_span[None, :]]  5.49 us
    dot_general x1, matrix products, shards(): jnp.einsum('bia,pabs->bpis', left, right, preferred_element_type=jnp.floa...  5.06 us
    reshape x2, local copies, waits for them, and re-layouts, shards(): term.reshape(nblk, pairs, width)  4.85 us
    dot_general x1, matrix products, shards(): jnp.einsum('pabs,bsn->pan', upper, right_rows, preferred_element_type=jnp...  4.45 us

commit v1 on v0

v1 whole, which is shorter than its diff:
```python
import functools

import jax
import jax.numpy as jnp
from jax import lax
from jax.experimental import pallas as pl
from jax.experimental.pallas import tpu as pltpu
from jax.sharding import PartitionSpec as P

SHELL_ROW = 8
SHELL_COL = 16
WIDTH = SHELL_ROW * SHELL_COL
GROUP = 2
SUB = 16
RIGHT_WIN = 32
LEFT_WIN = 16
LANES = 128
F32 = jnp.float32
BF16 = jnp.bfloat16
VMEM_LIMIT = 60 * 1024 * 1024


def iota(shape, dim):
    return lax.broadcasted_iota(jnp.int32, shape, dim)


def dot(a, b):
    return jnp.dot(a, b, preferred_element_type=F32)


def dot_t(a, b):
    return lax.dot_general(a, b, (((1,), (1,)), ((), ())), preferred_element_type=F32)


def chunk_of(pairs):
    return max(c for c in range(1, 6) if pairs % c == 0)


def window(low, size, nao):
    base = jnp.minimum(low // 8 * 8, nao - size)
    return pl.multiple_of(base, 8)


def back_kernel(
    nblk, ext_rows, offs, amp, virt, out, right_out, left_out, right_win, left_win, acc, sems
):
    nao, next_ = virt.shape
    first = lax.axis_index("sp") * ext_rows

    @pl.when(pl.program_id(0) == 0)
    def _():
        lane_base = pl.multiple_of(first // LANES * LANES, LANES)
        shift = first - lane_base
        copies = []
        for b in range(nblk):
            base = window(offs[1, b], RIGHT_WIN, nao)
            copies.append(
                pltpu.make_async_copy(
                    virt.at[pl.ds(base, RIGHT_WIN), :], right_win.at[b], sems.at[0, b]
                )
            )
            base = window(offs[0, b], LEFT_WIN, nao)
            copies.append(
                pltpu.make_async_copy(
                    virt.at[pl.ds(base, LEFT_WIN), pl.ds(lane_base, LANES)],
                    left_win.at[b],
                    sems.at[1, b],
                )
            )
        for copy in copies:
            copy.start()
        for copy in copies:
            copy.wait()
        half_sub = SUB // 2
        for g in range(nblk // half_sub):
            rows, cols = half_sub * SHELL_COL, half_sub * RIGHT_WIN
            row, col = iota((SHELL_COL, cols), 0), iota((SHELL_COL, cols), 1)
            parts = []
            for t in range(half_sub):
                low = offs[1, g * half_sub + t]
                delta = low - window(low, RIGHT_WIN, nao) + t * RIGHT_WIN
                parts.append(jnp.where(col == row + delta, 1.0, 0.0))
            pick = jnp.concatenate(parts, axis=0).astype(BF16)
            win = right_win[g * half_sub : (g + 1) * half_sub].reshape(cols, next_)
            right_out[g * rows : (g + 1) * rows, :] = dot(pick, win).astype(BF16)
        lane_pick = jnp.where(
            iota((LANES, ext_rows), 0) == iota((LANES, ext_rows), 1) + shift, 1.0, 0.0
        ).astype(BF16)
        for g in range(nblk // SUB):
            rows, cols = SUB * SHELL_ROW, SUB * LEFT_WIN
            row, col = iota((SHELL_ROW, cols), 0), iota((SHELL_ROW, cols), 1)
            parts = []
            for t in range(SUB):
                low = offs[0, g * SUB + t]
                delta = low - window(low, LEFT_WIN, nao) + t * LEFT_WIN
                parts.append(jnp.where(col == row + delta, 1.0, 0.0))
            pick = jnp.concatenate(parts, axis=0).astype(BF16)
            win = left_win[g * SUB : (g + 1) * SUB].reshape(cols, LANES)
            wide = dot(pick, win).astype(BF16)
            left_out[g * rows : (g + 1) * rows, :] = dot(wide, lane_pick).astype(BF16)

    chunk = amp.shape[0]
    half = dot_t(amp[...].reshape(chunk * ext_rows, next_), right_out[...]).astype(BF16)
    span = SUB * SHELL_COL
    block_of = iota((SHELL_ROW, span), 1) // SHELL_COL
    for q in range(chunk):
        own = half[q * ext_rows : (q + 1) * ext_rows]
        for g in range(nblk // SUB):
            left = left_out[g * SUB * SHELL_ROW : (g + 1) * SUB * SHELL_ROW, :]
            full = dot(left, own[:, g * span : (g + 1) * span])
            kept = full[:SHELL_ROW]
            for t in range(1, SUB):
                kept = jnp.where(
                    block_of == t, full[t * SHELL_ROW : (t + 1) * SHELL_ROW], kept
                )
            acc[q * SHELL_ROW : (q + 1) * SHELL_ROW, g * span : (g + 1) * span] = kept
    done = acc[...].astype(BF16)
    for copy in range(out.shape[0]):
        out[copy, 0] = done


def raw_kernel(slots, lists, live, got, *rest):
    slabs, out = rest[:-1], rest[-1]
    total = got[0].astype(F32)
    for src in range(1, got.shape[0]):
        total = total + got[src].astype(F32)
    ao = total.astype(BF16)
    rows, span = ao.shape
    cols = slots * SHELL_COL
    lane = iota((1, cols), 1)
    chosen = []
    for t in range(len(slabs)):
        target = jnp.full((1, cols), -1, jnp.int32)
        for k in range(slots):
            block = jnp.where(k < live[t, 0], lists[t, k], -nblk_guard(span))
            target = jnp.where(
                lane // SHELL_COL == k, block * SHELL_COL + lane % SHELL_COL, target
            )
        pick = jnp.where(iota((span, cols), 0) == target, 1.0, 0.0).astype(BF16)
        chosen.append(dot(ao, pick).astype(BF16))
    wide = slots * WIDTH
    down, across = iota((cols, wide), 0), iota((cols, wide), 1)
    spread = jnp.where(
        (down // SHELL_COL == across // WIDTH) & (down % SHELL_COL == across % SHELL_COL),
        1.0,
        0.0,
    ).astype(BF16)
    mask = iota((rows, wide), 0) % SHELL_ROW == iota((rows, wide), 1) % WIDTH // SHELL_COL
    pieces = []
    for t, slab in enumerate(slabs):
        laid = jnp.where(mask, dot(chosen[t], spread), 0.0).astype(BF16)
        raw = dot_t(laid, slab[...])
        pieces.append(jnp.sum(raw.reshape(rows // SHELL_ROW, SHELL_ROW, WIDTH), axis=1))
    done = jnp.concatenate(pieces, axis=0).astype(BF16)
    for copy in range(out.shape[0]):
        out[copy] = done


def nblk_guard(span):
    return span


def residual_kernel(
    groups, halves, nblk, ext_rows, raws, coupling, left, right, energies, amp, out, mixed, own_e
):
    pairs = coupling.shape[0]
    rows = raws.shape[1]
    each = rows // GROUP
    next_ = right.shape[1]

    @pl.when(pl.program_id(0) == 0)
    def _():
        first = lax.axis_index("sp") * ext_rows
        wide_e = energies[...]
        pick = iota((ext_rows, next_), 1) == iota((ext_rows, next_), 0) + first
        own_e[...] = jnp.sum(jnp.where(pick, wide_e, 0.0), axis=1, keepdims=True)
        couple = coupling[...]
        total = [None] * GROUP
        for member in range(GROUP):
            for h in range(halves):
                data = jnp.concatenate(
                    [raws[(g * GROUP + member) * halves + h] for g in range(groups)], axis=1
                )
                down, across = iota((couple.shape[1], rows), 0), iota((couple.shape[1], rows), 1)
                source = h * pairs + member * each + across % each
                for j in range(GROUP):
                    turn = (j - member) % GROUP
                    here = (down == source) & (across // each == turn)
                    weights = dot(couple, jnp.where(here, 1.0, 0.0).astype(BF16)).astype(BF16)
                    term = dot(weights, data)
                    total[j] = term if total[j] is None else total[j] + term
        for j in range(GROUP):
            done = total[j].astype(BF16).astype(F32)
            for c in range(mixed.shape[0]):
                mixed[c, j] = done[c * mixed.shape[2] : (c + 1) * mixed.shape[2]]

    chunk = amp.shape[0]
    span = SUB * SHELL_COL
    mask = iota((SHELL_ROW, WIDTH), 0) == iota((SHELL_ROW, WIDTH), 1) // SHELL_COL
    tile = jnp.where(
        iota((WIDTH, span), 0) % SHELL_COL == iota((WIDTH, span), 1) % SHELL_COL, 1.0, 0.0
    ).astype(BF16)
    high = SUB * SHELL_ROW
    diagonal = iota((high, span), 0) // SHELL_ROW == iota((high, span), 1) // SHELL_COL
    step = pl.program_id(0)
    uppers = []
    for q in range(chunk):
        columns = []
        for g in range(nblk // SUB):
            stack = []
            for t in range(SUB):
                b = g * SUB + t
                lanes = pl.ds(b // GROUP * WIDTH, WIDTH)
                row = mixed[step, b % GROUP, q : q + 1, lanes]
                stack.append(jnp.where(mask, jnp.broadcast_to(row, (SHELL_ROW, WIDTH)), 0.0))
            flat = jnp.concatenate(stack, axis=0).astype(BF16)
            square = jnp.where(diagonal, dot(flat, tile), 0.0).astype(BF16)
            part = left[g * high : (g + 1) * high, :]
            columns.append(
                lax.dot_general(part, square, (((0,), (0,)), ((), ())), preferred_element_type=F32)
            )
        uppers.append(jnp.concatenate(columns, axis=1).astype(BF16))
    upper = jnp.concatenate(uppers, axis=0)
    inner = dot(upper, right[...]).reshape(chunk, ext_rows, next_)
    diag = own_e[...] + energies[...]
    out[...] = (inner + diag[None] * amp[...].astype(F32)).astype(BF16)


def shards(amplitudes, virtuals, energies, integrals, screened, counts, offsets, coupling):
    pairs, ext_rows, next_ = amplitudes.shape
    nblk = offsets.shape[1]
    n = lax.axis_size("sp")
    halves = lax.axis_size("pb")
    slots = screened.shape[1]
    span = nblk * SHELL_COL
    each = pairs // GROUP
    rows = each * SHELL_ROW

    facts = jnp.concatenate([screened, counts[:, None]], axis=1)
    slabs, lists = [integrals], [facts]
    for turn in range(1, GROUP):
        ring = [
            (i // GROUP * GROUP + (i + turn) % GROUP, i) for i in range(n)
        ]
        slabs.append(lax.ppermute(integrals, "sp", ring))
        lists.append(lax.ppermute(facts, "sp", ring))
    facts = jnp.concatenate(lists, axis=0)

    chunk = chunk_of(each)
    smem = pl.BlockSpec(memory_space=pltpu.SMEM)
    vmem = pl.BlockSpec(memory_space=pltpu.VMEM)
    params = pltpu.CompilerParams(
        dimension_semantics=("arbitrary",), vmem_limit_bytes=VMEM_LIMIT
    )
    per = each // chunk
    partial, right, left = pl.pallas_call(
        functools.partial(back_kernel, nblk, ext_rows),
        grid=(pairs // chunk,),
        in_specs=[
            smem,
            pl.BlockSpec((chunk, ext_rows, next_), lambda c: (c, 0, 0)),
            pl.BlockSpec(memory_space=pltpu.HBM),
        ],
        out_specs=[
            pl.BlockSpec(
                (n // GROUP, 1, chunk * SHELL_ROW, span), lambda c: (0, c // per, c % per, 0)
            ),
            pl.BlockSpec((span, next_), lambda c: (0, 0)),
            pl.BlockSpec((nblk * SHELL_ROW, ext_rows), lambda c: (0, 0)),
        ],
        out_shape=[
            jax.ShapeDtypeStruct((n // GROUP, GROUP, rows, span), BF16),
            jax.ShapeDtypeStruct((span, next_), BF16),
            jax.ShapeDtypeStruct((nblk * SHELL_ROW, ext_rows), BF16),
        ],
        scratch_shapes=[
            pltpu.VMEM((nblk, RIGHT_WIN, next_), BF16),
            pltpu.VMEM((nblk, LEFT_WIN, LANES), BF16),
            pltpu.VMEM((chunk * SHELL_ROW, span), F32),
            pltpu.SemaphoreType.DMA((2, nblk)),
        ],
        compiler_params=params,
        name="back",
    )(offsets, amplitudes, virtuals)

    got = lax.all_to_all(partial.reshape(n, rows, span), "sp", 0, 0, tiled=True)

    raw = pl.pallas_call(
        functools.partial(raw_kernel, slots),
        in_specs=[smem, smem] + [vmem] * (1 + GROUP),
        out_specs=vmem,
        out_shape=jax.ShapeDtypeStruct((n * halves, GROUP * each, WIDTH), BF16),
        compiler_params=pltpu.CompilerParams(vmem_limit_bytes=VMEM_LIMIT),
        name="raw",
    )(facts[:, :slots], facts[:, slots:], got, *slabs)

    raws = lax.all_to_all(raw, ("sp", "pb"), 0, 0, tiled=True)

    return pl.pallas_call(
        functools.partial(residual_kernel, n // GROUP, halves, nblk, ext_rows),
        grid=(pairs // chunk,),
        in_specs=[
            pl.BlockSpec(raws.shape, lambda c: (0, 0, 0)),
            pl.BlockSpec(coupling.shape, lambda c: (0, 0)),
            pl.BlockSpec(left.shape, lambda c: (0, 0)),
            pl.BlockSpec(right.shape, lambda c: (0, 0)),
            pl.BlockSpec((1, next_), lambda c: (0, 0)),
            pl.BlockSpec((chunk, ext_rows, next_), lambda c: (c, 0, 0)),
        ],
        out_specs=pl.BlockSpec((chunk, ext_rows, next_), lambda c: (c, 0, 0)),
        out_shape=jax.ShapeDtypeStruct(amplitudes.shape, BF16),
        scratch_shapes=[
            pltpu.VMEM((pairs // chunk, GROUP, chunk, n // GROUP * WIDTH), F32),
            pltpu.VMEM((ext_rows, 1), F32),
        ],
        compiler_params=params,
        name="residual",
    )(raws, coupling, left, right, energies[None], amplitudes)


def solution(mesh):
    return jax.shard_map(
        shards,
        mesh=mesh,
        in_specs=(
            P("pb", "sp", None),
            P(),
            P(),
            P("sp", None),
            P("sp", None),
            P("sp"),
            P(),
            P("pb", None),
        ),
        out_specs=P("pb", "sp", None),
        check_vma=False,
    )
```

time: 169 us -> 63.6 us (0.38)
  blocking collectives: 117 us -> 13.6 us
  local copies, waits for them, and re-layouts: 30.2 us -> 1.64 us
  Pallas kernels: 0 us -> 18.8 us
  matrix products: 18.6 us -> 0 us
  waiting for transfers between devices: 0 us -> 17.8 us
  starting transfers between devices: 0 us -> 10.5 us
    psum x1 -> x0, blocking collectives: 80.3 us -> none  [shards(): lax.psum(term.reshape(nblk, pairs, width), 'sp').astype(jnp.bfloat16)]
    all_gather x1 -> x0, blocking collectives: 36.9 us -> none  [shards(): every = lax.all_gather(raw[None], ('sp', 'pb'), axis=0, tiled=True)]
    pallas_call x0 -> x3, Pallas kernels: none -> 18.8 us  [the longest x1 8.17 us: shards(): pl.pallas_call(functools.partial(residual_kernel, n // GROUP, halves, nbl...]
    dot_general x5 -> x0, matrix products: 18.6 us -> none  [the longest x1 7.57 us: shards(): jnp.einsum('pab,nb->pan', amplitudes, virtuals, preferred_element_type=jn...]
    ppermute x0 -> x2, waiting for transfers between devices: none -> 17.8 us  [the longest x1 17.8 us: shards(): lists.append(lax.ppermute(facts, 'sp', ring))]
    all_to_all x0 -> x1, blocking collectives: none -> 13.6 us  [shards(): raws = lax.all_to_all(raw, ('sp', 'pb'), 0, 0, tiled=True)]
    convert_element_type x2 -> x0, local copies, waits for them, and re-layouts: 11.4 us -> none  [the longest x1 10.8 us: shards(): half = jnp.einsum('pab,nb->pan', amplitudes, virtuals, preferred_element_...]
    gather x4 -> x0, local copies, waits for them, and re-layouts: 8.88 us -> none  [the longest x1 5.49 us: shards(): right = half[:, :, highs[:, None] + col_span[None, :]]]
  transfers between devices with their start and end apart: 0 -> 3, of which waited for: 0 -> 1; matrix products, arithmetic and copies ran while one was open for 0% -> 1% of each run, Pallas kernels for 0% -> 0%
where the time goes in v1:
time: 63.6 us; the launch traced here: 63.1 us
  Pallas kernels  18.8 us (30%)
  waiting for transfers between devices  17.8 us (28%)
  blocking collectives  13.6 us (21%)
  starting transfers between devices  10.5 us (17%)
  local copies, waits for them, and re-layouts  1.64 us (3%)
  between operations  0.71 us (1%)
    ppermute x1, waiting for transfers between devices, shards(): lists.append(lax.ppermute(facts, 'sp', ring))  17.8 us
    all_to_all x1, blocking collectives, shards(): raws = lax.all_to_all(raw, ('sp', 'pb'), 0, 0, tiled=True)  13.6 us
    all_to_all x1, starting transfers between devices, shards(): got = lax.all_to_all(partial.reshape(n, rows, span), 'sp', 0, 0, tiled=True)  8.37 us
    pallas_call x1, Pallas kernels, shards(): pl.pallas_call(functools.partial(residual_kernel, n // GROUP, halves, nbl...  8.17 us
    pallas_call x1, Pallas kernels, shards(): pl.pallas_call(functools.partial(back_kernel, nblk, ext_rows), grid=(pair...  7.37 us
    pallas_call x1, Pallas kernels, shards(): pl.pallas_call(functools.partial(raw_kernel, slots), in_specs=[smem, smem...  3.22 us
    ppermute x1, starting transfers between devices, shards(): slabs.append(lax.ppermute(integrals, 'sp', ring))  1.99 us
  transfers between devices with their start and end apart: 3, of which 1 were waited for; matrix products, arithmetic and copies ran while one was open for 1% of the time, Pallas kernels for 0%

profile of v1, /device:TPU:0, one launch (start us, length us, event | category | flops | bytes accessed | tf_op | source)
XLA Modules:
  0.0 63.1 jit_solution(17932594665451921817)
XLA Ops:
  0.0 0.0 copy-start.1
  0.0 0.0 copy-start.4
  0.0 7.4 %back.1 = (bf16[8,2,80,256]{3,2,1,0:T(8,128)(2,1)}, bf16[256,1024]{1,0:T(8,128)(2,1)}, bf16[128,64]{1,0:T(8,128)(2,1)}) custom-call(s32[2,16]{1,0:T(2,128)} %offs.1, bf16[20,64,1024]{2,1,0:T(8,128)(2,1)} %amp.3, bf16[1400,1024]{1,0:T(8,128)(2,1)} %virt.1), custom_call_target="tpu_custom_call" | custom-call | tf_op jit(solution)/shard_map/back/pallas_call | solution.py:256
  7.4 8.4 %all-to-all-start = ((bf16[16,80,256]{2,1,0:T(8,128)(2,1)}), bf16[16,80,256]{2,1,0:T(8,128)(2,1)S(1)}, u32[]{:S(2)}, u32[]{:S(2)}) async-start(bf16[16,80,256]{2,1,0:T(8,128)(2,1)} %bitcast.6), calls=%async_computation | async-start | bytes 1310720 | tf_op jit(solution)/shard_map/all_to_all | solution.py:286
  15.8 0.0 copy-done.1
  15.8 2.0 %collective-permute-start.1 = (bf16[128,2048]{1,0:T(8,128)(2,1)S(1)}, bf16[128,2048]{1,0:T(8,128)(2,1)S(1)}, u32[]{:S(2)}, u32[]{:S(2)}) collective-permute-start(bf16[128,2048]{1,0:T(8,128)(2,1)S(1)} %copy-done.1), channel_id=1, source_target_pairs={{2,0},{0,2},{6,4},{4,6},{10,8},{8,10},{14,12},{12,14},{18,16},{16,... | collective-permute-start | bytes 1572872 | tf_op jit(solution)/shard_map/ppermute | solution.py:245
  18.4 0.0 copy-done.4
  18.4 0.1 pad_add_fusion.1
  18.5 0.1 collective-permute-start
  18.6 17.8 %collective-permute-done = s32[1,17]{1,0:T(1,128)S(1)} collective-permute-done((s32[1,17]{1,0:T(1,128)S(1)}, s32[1,17]{1,0:T(1,128)S(1)}, u32[]{:S(2)}, u32[]{:S(2)}) %collective-permute-start) | collective-permute-done | bytes 100 | tf_op jit(solution)/shard_map/ppermute | solution.py:246
  36.4 0.1 pad_add_fusion
  36.4 0.0 copy-start.3
  36.5 0.6 %slice.7.live = s32[2,1]{1,0:T(2,128)} slice(s32[2,17]{1,0:T(2,128)S(1)} %pad_add_fusion), slice={[0:2], [16:17]} | slice | bytes 16 | tf_op jit(solution)/shard_map/slice | solution.py:295
  37.1 0.0 collective-permute-done.1.rest_1_
  37.1 0.0 copy-start.2
  37.1 0.0 all-to-all-done.got
  37.1 0.0 copy-start
  37.1 0.0 copy-done.3
  37.1 0.8 %copy-done.2 = bf16[128,2048]{1,0:T(8,128)(2,1)} copy-done((bf16[128,2048]{1,0:T(8,128)(2,1)}, bf16[128,2048]{1,0:T(8,128)(2,1)S(1)}, u32[]{:S(2)}) %copy-start.2) | copy-done | bytes 524312
  37.9 0.2 copy-done
  38.1 3.2 %raw.1 = bf16[32,20,128]{2,1,0:T(8,128)(2,1)} custom-call(s32[2,16]{1,0:T(2,128)} %bitcast.7, s32[2,1]{1,0:T(2,128)} %slice.7.live, bf16[16,80,256]{2,1,0:T(8,128)(2,1)} %copy-done, bf16[128,2048]{1,0:T(8,128)(2,1)} %rest_0_.1, bf16[128,2048]{1,0:T(8,128)(2,1)} %copy-done.2), custom_call_target="tpu_custom_call" | custom-call | tf_op jit(solution)/shard_map/raw/pallas_call | solution.py:288
  41.3 13.6 %all_to_all.10.raws = bf16[32,20,128]{2,1,0:T(8,128)(2,1)} all-to-all(bf16[32,20,128]{2,1,0:T(8,128)(2,1)} %raw.1), channel_id=1, replica_groups=mesh['sp'=16,'pb'=2] {'sp','pb'}, dimensions={0} | all-to-all | bytes 327680 | tf_op jit(solution)/shard_map/all_to_all | solution.py:297
  54.9 8.2 %residual.1 = bf16[20,64,1024]{2,1,0:T(8,128)(2,1)} custom-call(bf16[32,20,128]{2,1,0:T(8,128)(2,1)} %all_to_all.10.raws, bf16[20,40]{1,0:T(8,128)(2,1)} %coupling.1, bf16[128,64]{1,0:T(8,128)(2,1)} %get-tuple-element.9.left, bf16[256,1024]{1,0:T(8,128)(2,1)} %get-tuple-element.10.right, f32[1,1024]{1,0:T(1,128)} %bitcast.8, bf16[20,64,1024]{2,1,0:T(8,128)(2,1)} %amp.3), custom_call_target="tpu_custom_call" | custom-call | tf_op jit(solution)/shard_map/residual/pallas_call | solution.py:299
Async XLA Ops:
  0.0 15.8 %copy-start.1 = (bf16[128,2048]{1,0:T(8,128)(2,1)S(1)}, bf16[128,2048]{1,0:T(8,128)(2,1)}, u32[]{:S(2)}) copy-start(bf16[128,2048]{1,0:T(8,128)(2,1)} %rest_0_.1) | copy-start | bytes 1572868
  0.0 18.4 %copy-start.4 = (s32[1,16]{1,0:T(1,128)S(1)}, s32[1,16]{1,0:T(1,128)}, u32[]{:S(2)}) copy-start(s32[1,16]{1,0:T(1,128)} %param.12) | copy-start | bytes 196
  7.4 29.7 %all-to-all-start = ((bf16[16,80,256]{2,1,0:T(8,128)(2,1)}), bf16[16,80,256]{2,1,0:T(8,128)(2,1)S(1)}, u32[]{:S(2)}, u32[]{:S(2)}) async-start(bf16[16,80,256]{2,1,0:T(8,128)(2,1)} %bitcast.6), calls=%async_computation | async-start | bytes 1310720 | tf_op jit(solution)/shard_map/all_to_all | solution.py:286
  15.8 21.3 %collective-permute-start.1 = (bf16[128,2048]{1,0:T(8,128)(2,1)S(1)}, bf16[128,2048]{1,0:T(8,128)(2,1)S(1)}, u32[]{:S(2)}, u32[]{:S(2)}) collective-permute-start(bf16[128,2048]{1,0:T(8,128)(2,1)S(1)} %copy-done.1), channel_id=1, source_target_pairs={{2,0},{0,2},{6,4},{4,6},{10,8},{8,10},{14,12},{12,14},{18,16},{16,... | collective-permute-start | bytes 1572872 | tf_op jit(solution)/shard_map/ppermute | solution.py:245
  18.5 17.9 %collective-permute-start = (s32[1,17]{1,0:T(1,128)S(1)}, s32[1,17]{1,0:T(1,128)S(1)}, u32[]{:S(2)}, u32[]{:S(2)}) collective-permute-start(s32[1,17]{1,0:T(1,128)S(1)} %pad_add_fusion.1), channel_id=1, source_target_pairs={{2,0},{0,2},{6,4},{4,6},{10,8},{8,10},{14,12},{12,14},{18,16},{16,... | collective-permute-start | bytes 212 | tf_op jit(solution)/shard_map/ppermute | solution.py:246
  36.4 0.7 %copy-start.3 = (s32[2,17]{1,0:T(2,128)}, s32[2,17]{1,0:T(2,128)S(1)}, u32[]{:S(2)}) copy-start(s32[2,17]{1,0:T(2,128)S(1)} %pad_add_fusion) | copy-start | bytes 412
  37.1 0.8 %copy-start.2 = (bf16[128,2048]{1,0:T(8,128)(2,1)}, bf16[128,2048]{1,0:T(8,128)(2,1)S(1)}, u32[]{:S(2)}) copy-start(bf16[128,2048]{1,0:T(8,128)(2,1)S(1)} %collective-permute-done.1.rest_1_) | copy-start | bytes 1572868
  37.1 1.0 %copy-start = (bf16[16,80,256]{2,1,0:T(8,128)(2,1)}, bf16[16,80,256]{2,1,0:T(8,128)(2,1)S(1)}, u32[]{:S(2)}) copy-start(bf16[16,80,256]{2,1,0:T(8,128)(2,1)S(1)} %all-to-all-done.got) | copy-start | bytes 1966084

commit v2 on v1

--- a/solution.py
+++ b/solution.py
@@ -17,7 +17,6 @@
 LANES = 128
 F32 = jnp.float32
 BF16 = jnp.bfloat16
-VMEM_LIMIT = 60 * 1024 * 1024
 
 
 def iota(shape, dim):
@@ -132,7 +131,7 @@
     for t in range(len(slabs)):
         target = jnp.full((1, cols), -1, jnp.int32)
         for k in range(slots):
-            block = jnp.where(k < live[t, 0], lists[t, k], -nblk_guard(span))
+            block = jnp.where(k < live[t, 0], lists[t, k], -span)
             target = jnp.where(
                 lane // SHELL_COL == k, block * SHELL_COL + lane % SHELL_COL, target
             )
@@ -154,10 +153,6 @@
     done = jnp.concatenate(pieces, axis=0).astype(BF16)
     for copy in range(out.shape[0]):
         out[copy] = done
-
-
-def nblk_guard(span):
-    return span
 
 
 def residual_kernel(
@@ -249,11 +244,12 @@
     chunk = chunk_of(each)
     smem = pl.BlockSpec(memory_space=pltpu.SMEM)
     vmem = pl.BlockSpec(memory_space=pltpu.VMEM)
+    grant = min(60, nblk) * 1024 * 1024
     params = pltpu.CompilerParams(
-        dimension_semantics=("arbitrary",), vmem_limit_bytes=VMEM_LIMIT
+        dimension_semantics=("arbitrary",), vmem_limit_bytes=grant
     )
     per = each // chunk
-    partial, right, left = pl.pallas_call(
+    back = pl.pallas_call(
         functools.partial(back_kernel, nblk, ext_rows),
         grid=(pairs // chunk,),
         in_specs=[
@@ -279,9 +275,12 @@
             pltpu.VMEM((chunk * SHELL_ROW, span), F32),
             pltpu.SemaphoreType.DMA((2, nblk)),
         ],
-        compiler_params=params,
+        compiler_params=pltpu.CompilerParams(
+            dimension_semantics=("arbitrary",), vmem_limit_bytes=60 * 1024 * 1024
+        ),
         name="back",
-    )(offsets, amplitudes, virtuals)
+    )
+    partial, right, left = back(offsets, amplitudes, virtuals)
 
     got = lax.all_to_all(partial.reshape(n, rows, span), "sp", 0, 0, tiled=True)
 
@@ -290,7 +289,7 @@
         in_specs=[smem, smem] + [vmem] * (1 + GROUP),
         out_specs=vmem,
         out_shape=jax.ShapeDtypeStruct((n * halves, GROUP * each, WIDTH), BF16),
-        compiler_params=pltpu.CompilerParams(vmem_limit_bytes=VMEM_LIMIT),
+        compiler_params=pltpu.CompilerParams(vmem_limit_bytes=grant),
         name="raw",
     )(facts[:, :slots], facts[:, slots:], got, *slabs)
 

time: 63.6 us -> 62.5 us (0.983)
  Pallas kernels: 18.8 us -> 15.7 us
  local copies, waits for them, and re-layouts: 1.64 us -> 3.72 us
    unnamed x10 -> x18, local copies, waits for them, and re-layouts: 1 us -> 3.65 us
    pallas_call x1, Pallas kernels: 8.17 us -> 6.64 us  [shards(): pl.pallas_call(functools.partial(residual_kernel, n // GROUP, halves, nbl...]
    pallas_call x1, Pallas kernels: 3.22 us -> 1.7 us  [shards(): pl.pallas_call(functools.partial(raw_kernel, slots), in_specs=[smem, smem...]
  transfers between devices with their start and end apart: 3 -> 3, of which waited for: 1 -> 1; matrix products, arithmetic and copies ran while one was open for 1% -> 0% of each run, Pallas kernels for 0% -> 0%
where the time goes in v2:
time: 62.5 us; the launch traced here: 61.9 us
  waiting for transfers between devices  17.8 us (28%)
  Pallas kernels  15.7 us (25%)
  blocking collectives  13.3 us (21%)
  starting transfers between devices  10.6 us (17%)
  local copies, waits for them, and re-layouts  3.72 us (6%)
  between operations  0.72 us (1%)
    ppermute x1, waiting for transfers between devices, shards(): lists.append(lax.ppermute(facts, 'sp', ring))  17.8 us
    all_to_all x1, blocking collectives, shards(): raws = lax.all_to_all(raw, ('sp', 'pb'), 0, 0, tiled=True)  13.3 us
    all_to_all x1, starting transfers between devices, shards(): got = lax.all_to_all(partial.reshape(n, rows, span), 'sp', 0, 0, tiled=True)  8.49 us
    pallas_call x1, Pallas kernels, shards(): partial, right, left = back(offsets, amplitudes, virtuals)  7.35 us
    pallas_call x1, Pallas kernels, shards(): pl.pallas_call(functools.partial(residual_kernel, n // GROUP, halves, nbl...  6.64 us
    unnamed x18, local copies, waits for them, and re-layouts  3.65 us
    ppermute x1, starting transfers between devices, shards(): slabs.append(lax.ppermute(integrals, 'sp', ring))  1.93 us
    pallas_call x1, Pallas kernels, shards(): pl.pallas_call(functools.partial(raw_kernel, slots), in_specs=[smem, smem...  1.7 us
  transfers between devices with their start and end apart: 3, of which 1 were waited for; matrix products, arithmetic and copies ran while one was open for 0% of the time, Pallas kernels for 0%

profile of v2, /device:TPU:0, one launch (start us, length us, event | category | flops | bytes accessed | tf_op | source)
XLA Modules:
  0.0 61.9 jit_solution(2566966079363199053)
XLA Ops:
  0.0 7.4 %back.1 = (bf16[8,2,80,256]{3,2,1,0:T(8,128)(2,1)}, bf16[256,1024]{1,0:T(8,128)(2,1)}, bf16[128,64]{1,0:T(8,128)(2,1)}) custom-call(s32[2,16]{1,0:T(2,128)} %offs.1, bf16[20,64,1024]{2,1,0:T(8,128)(2,1)} %amp.3, bf16[1400,1024]{1,0:T(8,128)(2,1)} %virt.1), custom_call_target="tpu_custom_call" | custom-call | tf_op jit(solution)/shard_map/back/pallas_call | solution.py:283
  7.4 0.0 copy-start
  7.4 8.5 %all-to-all-start = ((bf16[16,80,256]{2,1,0:T(8,128)(2,1)}), bf16[16,80,256]{2,1,0:T(8,128)(2,1)S(1)}, u32[]{:S(2)}, u32[]{:S(2)}) async-start(bf16[16,80,256]{2,1,0:T(8,128)(2,1)} %bitcast.8), calls=%async_computation | async-start | bytes 1310720 | tf_op jit(solution)/shard_map/all_to_all | solution.py:285
  15.9 1.9 %collective-permute-start.1 = (bf16[128,2048]{1,0:T(8,128)(2,1)}, bf16[128,2048]{1,0:T(8,128)(2,1)S(1)}, u32[]{:S(2)}, u32[]{:S(2)}) collective-permute-start(bf16[128,2048]{1,0:T(8,128)(2,1)} %rest_0_.1), channel_id=1, source_target_pairs={{2,0},{0,2},{6,4},{4,6},{10,8},{8,10},{14,12},{12,14},{18,16},{16,... | collective-permute-start | bytes 1572872 | tf_op jit(solution)/shard_map/ppermute | solution.py:240
  18.4 0.0 copy-done.8
  18.5 0.1 pad_add_fusion.1
  18.5 0.2 collective-permute-start
  18.7 17.8 %collective-permute-done = s32[1,17]{1,0:T(1,128)S(1)} collective-permute-done((s32[1,17]{1,0:T(1,128)S(1)}, s32[1,17]{1,0:T(1,128)S(1)}, u32[]{:S(2)}, u32[]{:S(2)}) %collective-permute-start) | collective-permute-done | bytes 100 | tf_op jit(solution)/shard_map/ppermute | solution.py:241
  36.5 0.1 pad_add_fusion
  36.6 0.1 slice.7.live
  36.6 0.0 collective-permute-done.1.rest_1_
  36.6 0.8 %copy-done.2 = bf16[128,2048]{1,0:T(8,128)(2,1)} copy-done((bf16[128,2048]{1,0:T(8,128)(2,1)}, bf16[128,2048]{1,0:T(8,128)(2,1)S(1)}, u32[]{:S(2)}) %copy-start.2) | copy-done | bytes 524312
  37.4 0.0 all-to-all-done.got
  37.4 1.0 %copy-done.1 = bf16[128,2048]{1,0:T(8,128)(2,1)S(1)} copy-done((bf16[128,2048]{1,0:T(8,128)(2,1)S(1)}, bf16[128,2048]{1,0:T(8,128)(2,1)}, u32[]{:S(2)}) %copy-start.1) | copy-done | bytes 524312
  38.5 1.0 %copy-done.3 = bf16[128,2048]{1,0:T(8,128)(2,1)S(1)} copy-done((bf16[128,2048]{1,0:T(8,128)(2,1)S(1)}, bf16[128,2048]{1,0:T(8,128)(2,1)}, u32[]{:S(2)}) %copy-start.3) | copy-done | bytes 524312
  39.5 1.7 %raw.1 = bf16[32,20,128]{2,1,0:T(8,128)(2,1)S(1)} custom-call(s32[2,16]{1,0:T(2,128)S(1)} %bitcast.6, s32[2,1]{1,0:T(2,128)S(1)} %slice.7.live, bf16[16,80,256]{2,1,0:T(8,128)(2,1)S(1)} %all-to-all-done.got, bf16[128,2048]{1,0:T(8,128)(2,1)S(1)} %copy-done.1, bf16[128,2048]{1,0:T(8,128)(2,1)S(1)} %copy-done.3), custom_call_target="tpu_custom_call" | custom-call | tf_op jit(solution)/shard_map/raw/pallas_call | solution.py:287
  41.2 13.3 %all_to_all.10.raws = bf16[32,20,128]{2,1,0:T(8,128)(2,1)S(1)} all-to-all(bf16[32,20,128]{2,1,0:T(8,128)(2,1)S(1)} %raw.1), channel_id=1, replica_groups=mesh['sp'=16,'pb'=2] {'sp','pb'}, dimensions={0} | all-to-all | bytes 327680 | tf_op jit(solution)/shard_map/all_to_all | solution.py:296
  54.5 0.0 copy-done.6
  54.5 0.0 copy-done.7
  54.5 0.0 copy-done
  54.5 0.0 copy-done.4
  54.5 0.0 copy-start.5
  54.5 0.7 %copy-done.5 = bf16[128,64]{1,0:T(8,128)(2,1)S(1)} copy-done((bf16[128,64]{1,0:T(8,128)(2,1)S(1)}, bf16[128,64]{1,0:T(8,128)(2,1)}, u32[]{:S(2)}) %copy-start.5) | copy-done | bytes 16408
  55.3 6.6 %residual.1 = bf16[20,64,1024]{2,1,0:T(8,128)(2,1)} custom-call(bf16[32,20,128]{2,1,0:T(8,128)(2,1)S(1)} %all_to_all.10.raws, bf16[20,40]{1,0:T(8,128)(2,1)S(1)} %copy-done.6, bf16[128,64]{1,0:T(8,128)(2,1)S(1)} %copy-done.5, bf16[256,1024]{1,0:T(8,128)(2,1)S(1)} %copy-done.4, f32[1,1024]{1,0:T(1,128)S(1)} %bitcast.7, bf16[20,64,1024]{2,1,0:T(8,128)(2,1)S(1)} %copy-done), custom_call_target="tpu_custom_call" | custom-call | tf_op jit(solution)/shard_map/residual/pallas_call | solution.py:298
  (7 shorter events, 0.0 us)
Async XLA Ops:
  0.0 18.5 %copy-start.8 = (s32[1,16]{1,0:T(1,128)S(1)}, s32[1,16]{1,0:T(1,128)}, u32[]{:S(2)}) copy-start(s32[1,16]{1,0:T(1,128)} %param.12) | copy-start | bytes 196
  0.0 54.5 %copy-start.6 = (bf16[20,40]{1,0:T(8,128)(2,1)S(1)}, bf16[20,40]{1,0:T(8,128)(2,1)}, u32[]{:S(2)}) copy-start(bf16[20,40]{1,0:T(8,128)(2,1)} %coupling.1) | copy-start | bytes 4804
  0.0 54.5 %copy-start.7 = (f32[1024]{0:T(1024)S(1)}, f32[1024]{0:T(1024)}, u32[]{:S(2)}) copy-start(f32[1024]{0:T(1024)} %param.10) | copy-start | bytes 12292
  7.4 47.2 %copy-start = (bf16[20,64,1024]{2,1,0:T(8,128)(2,1)S(1)}, bf16[20,64,1024]{2,1,0:T(8,128)(2,1)}, u32[]{:S(2)}) copy-start(bf16[20,64,1024]{2,1,0:T(8,128)(2,1)} %amp.3) | copy-start | bytes 7864324
  7.4 30.0 %all-to-all-start = ((bf16[16,80,256]{2,1,0:T(8,128)(2,1)}), bf16[16,80,256]{2,1,0:T(8,128)(2,1)S(1)}, u32[]{:S(2)}, u32[]{:S(2)}) async-start(bf16[16,80,256]{2,1,0:T(8,128)(2,1)} %bitcast.8), calls=%async_computation | async-start | bytes 1310720 | tf_op jit(solution)/shard_map/all_to_all | solution.py:285
  15.9 20.8 %collective-permute-start.1 = (bf16[128,2048]{1,0:T(8,128)(2,1)}, bf16[128,2048]{1,0:T(8,128)(2,1)S(1)}, u32[]{:S(2)}, u32[]{:S(2)}) collective-permute-start(bf16[128,2048]{1,0:T(8,128)(2,1)} %rest_0_.1), channel_id=1, source_target_pairs={{2,0},{0,2},{6,4},{4,6},{10,8},{8,10},{14,12},{12,14},{18,16},{16,... | collective-permute-start | bytes 1572872 | tf_op jit(solution)/shard_map/ppermute | solution.py:240
  18.5 17.9 %collective-permute-start = (s32[1,17]{1,0:T(1,128)S(1)}, s32[1,17]{1,0:T(1,128)S(1)}, u32[]{:S(2)}, u32[]{:S(2)}) collective-permute-start(s32[1,17]{1,0:T(1,128)S(1)} %pad_add_fusion.1), channel_id=1, source_target_pairs={{2,0},{0,2},{6,4},{4,6},{10,8},{8,10},{14,12},{12,14},{18,16},{16,... | collective-permute-start | bytes 212 | tf_op jit(solution)/shard_map/ppermute | solution.py:241
  36.6 0.8 %copy-start.2 = (bf16[128,2048]{1,0:T(8,128)(2,1)}, bf16[128,2048]{1,0:T(8,128)(2,1)S(1)}, u32[]{:S(2)}) copy-start(bf16[128,2048]{1,0:T(8,128)(2,1)S(1)} %collective-permute-done.1.rest_1_) | copy-start | bytes 1572868
  37.4 1.0 %copy-start.1 = (bf16[128,2048]{1,0:T(8,128)(2,1)S(1)}, bf16[128,2048]{1,0:T(8,128)(2,1)}, u32[]{:S(2)}) copy-start(bf16[128,2048]{1,0:T(8,128)(2,1)} %rest_0_.1) | copy-start | bytes 1572868
  38.5 1.0 %copy-start.3 = (bf16[128,2048]{1,0:T(8,128)(2,1)S(1)}, bf16[128,2048]{1,0:T(8,128)(2,1)}, u32[]{:S(2)}) copy-start(bf16[128,2048]{1,0:T(8,128)(2,1)} %copy-done.2) | copy-start | bytes 1572868
  39.5 15.0 %copy-start.4 = (bf16[256,1024]{1,0:T(8,128)(2,1)S(1)}, bf16[256,1024]{1,0:T(8,128)(2,1)}, u32[]{:S(2)}) copy-start(bf16[256,1024]{1,0:T(8,128)(2,1)} %get-tuple-element.10.right) | copy-start | bytes 1572868
  54.5 0.8 %copy-start.5 = (bf16[128,64]{1,0:T(8,128)(2,1)S(1)}, bf16[128,64]{1,0:T(8,128)(2,1)}, u32[]{:S(2)}) copy-start(bf16[128,64]{1,0:T(8,128)(2,1)} %get-tuple-element.9.left) | copy-start | bytes 49156

commit v3 on v0

v3 whole, which is shorter than its diff:
```python
import functools

import jax
import jax.numpy as jnp
from jax import lax
from jax.experimental import pallas as pl
from jax.experimental.pallas import tpu as pltpu
from jax.sharding import PartitionSpec as P

SHELL_ROW = 8
SHELL_COL = 16
WIDTH = SHELL_ROW * SHELL_COL
SUB = 16
RIGHT_WIN = 32
LEFT_WIN = 16
LANES = 128
PACK = 32
F32 = jnp.float32
BF16 = jnp.bfloat16
VMEM = pl.BlockSpec(memory_space=pltpu.VMEM)
HBM = pl.BlockSpec(memory_space=pltpu.HBM)


def iota(shape, dim):
    return lax.broadcasted_iota(jnp.int32, shape, dim)


def dot(a, b):
    return jnp.dot(a, b, preferred_element_type=F32)


def dot_t(a, b):
    return lax.dot_general(a, b, (((1,), (1,)), ((), ())), preferred_element_type=F32)


def chunk_of(pairs):
    return max(c for c in range(1, 6) if pairs % c == 0)


def window(low, size, nao):
    base = jnp.minimum(low // 8 * 8, nao - size)
    return pl.multiple_of(base, 8)


def picks(offs, which, first, count, shell, size, nao):
    cols = count * size
    row, col = iota((shell, cols), 0), iota((shell, cols), 1)
    parts = []
    for t in range(count):
        low = offs[which, first + t]
        delta = low - window(low, size, nao) + t * size
        parts.append(jnp.where(col == row + delta, 1.0, 0.0))
    return jnp.concatenate(parts, axis=0).astype(BF16)


def back_kernel(
    nblk, chunk, offs_in, lists_in, live, amp, virt, slab, out, right, left, amps, slab_out, pick_out,
    offs, lists, right_win, left_win, acc, sems, amp_sems
):
    pairs, ext_rows, next_ = amp.shape
    nao = virt.shape[0]
    first = lax.axis_index("sp") * ext_rows
    lane_base = pl.multiple_of(first // LANES * LANES, LANES)
    shift = first - lane_base
    rights, lefts, loads = [], [], []
    facts = [
        pltpu.make_async_copy(offs_in, offs, amp_sems.at[pairs // chunk + 1]),
        pltpu.make_async_copy(lists_in, lists, amp_sems.at[pairs // chunk + 2]),
    ]
    for fact in facts:
        fact.start()
    facts[0].wait()
    for b in range(nblk):
        base = window(offs[1, b], RIGHT_WIN, nao)
        rights.append(
            pltpu.make_async_copy(
                virt.at[pl.ds(base, RIGHT_WIN), :], right_win.at[b], sems.at[0, b]
            )
        )
        rights[-1].start()
    for c in range(pairs // chunk):
        span_c = pl.ds(c * chunk, chunk)
        loads.append(pltpu.make_async_copy(amp.at[span_c], amps.at[span_c], amp_sems.at[c]))
    loads[0].start()
    for b in range(nblk):
        base = window(offs[0, b], LEFT_WIN, nao)
        lefts.append(
            pltpu.make_async_copy(
                virt.at[pl.ds(base, LEFT_WIN), pl.ds(lane_base, LANES)],
                left_win.at[b],
                sems.at[1, b],
            )
        )
        lefts[-1].start()
    for load in loads[1:]:
        load.start()
    slab_load = pltpu.make_async_copy(slab, slab_out, amp_sems.at[pairs // chunk])
    slab_load.start()
    half_sub = SUB // 2
    rows, cols = half_sub * SHELL_COL, half_sub * RIGHT_WIN
    for g in range(nblk // half_sub):
        pick = picks(offs, 1, g * half_sub, half_sub, SHELL_COL, RIGHT_WIN, nao)
        for b in range(g * half_sub, (g + 1) * half_sub):
            rights[b].wait()
        win = right_win[g * half_sub : (g + 1) * half_sub].reshape(cols, next_)
        right[g * rows : (g + 1) * rows, :] = dot(pick, win).astype(BF16)
    lane_pick = jnp.where(
        iota((LANES, ext_rows), 0) == iota((LANES, ext_rows), 1) + shift, 1.0, 0.0
    ).astype(BF16)
    high = SUB * SHELL_ROW
    for g in range(nblk // SUB):
        pick = picks(offs, 0, g * SUB, SUB, SHELL_ROW, LEFT_WIN, nao)
        for b in range(g * SUB, (g + 1) * SUB):
            lefts[b].wait()
        win = left_win[g * SUB : (g + 1) * SUB].reshape(SUB * LEFT_WIN, LANES)
        wide = dot(pick, win).astype(BF16)
        left[g * high : (g + 1) * high, :] = dot(wide, lane_pick).astype(BF16)

    span = SUB * SHELL_COL
    block_of = iota((SHELL_ROW, span), 1) // SHELL_COL
    for c in range(pairs // chunk):
        loads[c].wait()
        data = amps[c * chunk : (c + 1) * chunk].reshape(chunk * ext_rows, next_)
        half = dot_t(data, right[...]).astype(BF16)
        for q in range(chunk):
            own = half[q * ext_rows : (q + 1) * ext_rows]
            for g in range(nblk // SUB):
                full = dot(left[g * high : (g + 1) * high, :], own[:, g * span : (g + 1) * span])
                kept = full[:SHELL_ROW]
                for t in range(1, SUB):
                    kept = jnp.where(
                        block_of == t, full[t * SHELL_ROW : (t + 1) * SHELL_ROW], kept
                    )
                acc[:, c * chunk + q, g * span : (g + 1) * span] = kept
    tiles = nblk * SHELL_COL // LANES
    for i in range(SHELL_ROW):
        for t in range(tiles):
            done = acc[i, :, t * LANES : (t + 1) * LANES].astype(BF16)
            for h in range(out.shape[1]):
                out[i * tiles + t, h] = done
    for fact in facts[1:]:
        fact.wait()
    slots = lists.shape[1]
    whole, cols = nblk * SHELL_COL, slots * SHELL_COL
    lane = iota((1, cols), 1)
    target = jnp.full((1, cols), -1, jnp.int32)
    for k in range(slots):
        block = jnp.where(k < live[0], lists[0, k], -whole)
        target = jnp.where(
            lane // SHELL_COL == k, block * SHELL_COL + lane % SHELL_COL, target
        )
    pick_out[...] = jnp.where(iota((whole, cols), 0) == target, 1.0, 0.0).astype(BF16)
    slab_load.wait()


def mix_kernel(n, halves, got, coupling, out):
    pairs = coupling.shape[0]
    sums = []
    for h in range(halves):
        total = got[h].astype(F32)
        for s in range(1, n):
            total = total + got[s * halves + h].astype(F32)
        sums.append(total)
    ao = jnp.concatenate(sums, axis=0).astype(BF16)
    mixed = dot(coupling[...], ao).astype(BF16)
    for d in range(n):
        out[d, :pairs] = mixed
        out[d, pairs:] = jnp.zeros((out.shape[1] - pairs, LANES), BF16)


def raw_kernel(pairs, pick, got, slab, out):
    n, rows, _ = got.shape
    tiles = n // SHELL_ROW
    cols = pick.shape[1]
    slots = cols // SHELL_COL
    held = got[...].reshape(SHELL_ROW, tiles, rows, LANES)
    ao = jnp.concatenate(
        [held[:, t].reshape(SHELL_ROW * rows, LANES) for t in range(tiles)], axis=1
    )
    chosen = dot(ao, pick[...])
    need = -(-pairs // 8) * 8
    per = LANES // SHELL_COL
    group = iota((need, LANES), 1) // SHELL_COL
    turned = {}
    for i in range(SHELL_ROW):
        for t in range(cols // LANES):
            tile = chosen[i * rows : i * rows + need, t * LANES : (t + 1) * LANES]
            for m in range(per):
                turned[i, t, m] = pltpu.roll(tile, m * SHELL_COL, 1) if m else tile
    laid = []
    for k in range(slots):
        t, at = k // per, k % per
        piece = turned[0, t, (0 - at) % per]
        for i in range(1, SHELL_ROW):
            piece = jnp.where(group == i, turned[i, t, (i - at) % per], piece)
        laid.append(piece)
    raw = dot_t(jnp.concatenate(laid, axis=1).astype(BF16), slab[...])
    done = raw[:pairs].astype(BF16)
    for d in range(n):
        out[d] = done


def residual_kernel(nblk, ext_rows, raws, left, right, energies, amp, out, mixed, own_e):
    pairs = raws.shape[1]
    next_ = right.shape[1]

    @pl.when(pl.program_id(0) == 0)
    def _():
        first = lax.axis_index("sp") * ext_rows
        lane_base = pl.multiple_of(first // LANES * LANES, LANES)
        near = energies[:, pl.ds(lane_base, LANES)]
        pick = iota((ext_rows, LANES), 1) == iota((ext_rows, LANES), 0) + (first - lane_base)
        own_e[...] = jnp.sum(jnp.where(pick, near, 0.0), axis=1, keepdims=True)
        for b in range(nblk):
            mixed[:, b, :] = raws[b].astype(F32)

    chunk = amp.shape[0]
    span = SUB * SHELL_COL
    high = SUB * SHELL_ROW
    mask = iota((SUB, SHELL_ROW, WIDTH), 1) == iota((SUB, SHELL_ROW, WIDTH), 2) // SHELL_COL
    tile = jnp.where(
        iota((WIDTH, span), 0) % SHELL_COL == iota((WIDTH, span), 1) % SHELL_COL, 1.0, 0.0
    ).astype(BF16)
    diagonal = iota((high, span), 0) // SHELL_ROW == iota((high, span), 1) // SHELL_COL
    base = pl.program_id(0) * chunk
    uppers = []
    for q in range(chunk):
        columns = []
        for g in range(nblk // SUB):
            block = mixed[base + q, g * SUB : (g + 1) * SUB, :]
            flat = jnp.where(mask, block[:, None, :], 0.0).reshape(high, WIDTH).astype(BF16)
            square = jnp.where(diagonal, dot(flat, tile), 0.0).astype(BF16)
            part = left[g * high : (g + 1) * high, :]
            columns.append(
                lax.dot_general(part, square, (((0,), (0,)), ((), ())), preferred_element_type=F32)
            )
        uppers.append(jnp.concatenate(columns, axis=1).astype(BF16))
    upper = jnp.concatenate(uppers, axis=0)
    inner = dot(upper, right[...]).reshape(chunk, ext_rows, next_)
    diag = own_e[...] + energies[...]
    out[...] = (inner + diag[None] * amp[...].astype(F32)).astype(BF16)


def shards(amplitudes, virtuals, energies, integrals, screened, counts, offsets, coupling):
    pairs, ext_rows, next_ = amplitudes.shape
    nblk = offsets.shape[1]
    n = lax.axis_size("sp")
    halves = lax.axis_size("pb")
    slots = screened.shape[1]
    span = nblk * SHELL_COL
    chunk = chunk_of(pairs)
    padded = -(-pairs // PACK) * PACK
    plain = pltpu.CompilerParams(vmem_limit_bytes=min(60, nblk) * 1024 * 1024)
    in_hbm = functools.partial(
        pltpu.with_memory_space_constraint, memory_space=pltpu.HBM
    )

    partial, right, left, held, slab, pick = pl.pallas_call(
        functools.partial(back_kernel, nblk, chunk),
        in_specs=[HBM, HBM, pl.BlockSpec(memory_space=pltpu.SMEM), HBM, HBM, HBM],
        out_specs=[VMEM] * 6,
        out_shape=[
            jax.ShapeDtypeStruct((n, halves, pairs, LANES), BF16),
            jax.ShapeDtypeStruct((span, next_), BF16),
            jax.ShapeDtypeStruct((nblk * SHELL_ROW, ext_rows), BF16),
            jax.ShapeDtypeStruct(amplitudes.shape, BF16),
            jax.ShapeDtypeStruct(integrals.shape, BF16),
            jax.ShapeDtypeStruct((span, slots * SHELL_COL), BF16),
        ],
        scratch_shapes=[
            pltpu.SMEM(offsets.shape, jnp.int32),
            pltpu.SMEM(screened.shape, jnp.int32),
            pltpu.VMEM((nblk, RIGHT_WIN, next_), BF16),
            pltpu.VMEM((nblk, LEFT_WIN, LANES), BF16),
            pltpu.VMEM((SHELL_ROW, pairs, span), F32),
            pltpu.SemaphoreType.DMA((2, nblk)),
            pltpu.SemaphoreType.DMA((pairs // chunk + 4,)),
        ],
        compiler_params=plain,
        name="back",
    )(in_hbm(offsets), in_hbm(screened), counts, in_hbm(amplitudes), in_hbm(virtuals), in_hbm(integrals))

    got = lax.all_to_all(
        partial.reshape(n * halves, pairs, LANES), ("sp", "pb"), 0, 0, tiled=True
    )
    ao = pl.pallas_call(
        functools.partial(mix_kernel, n, halves),
        in_specs=[VMEM, VMEM],
        out_specs=VMEM,
        out_shape=jax.ShapeDtypeStruct((n, padded, LANES), BF16),
        compiler_params=plain,
        name="mix",
    )(got, coupling)

    ao_all = lax.all_to_all(ao, "sp", 0, 0, tiled=True)
    raw = pl.pallas_call(
        functools.partial(raw_kernel, pairs),
        in_specs=[VMEM] * 3,
        out_specs=VMEM,
        out_shape=jax.ShapeDtypeStruct((n, pairs, WIDTH), BF16),
        compiler_params=plain,
        name="raw",
    )(pick, ao_all, slab)

    raws = lax.all_to_all(raw, "sp", 0, 0, tiled=True)
    return pl.pallas_call(
        functools.partial(residual_kernel, nblk, ext_rows),
        grid=(pairs // chunk,),
        in_specs=[
            pl.BlockSpec(raws.shape, lambda c: (0, 0, 0)),
            pl.BlockSpec(left.shape, lambda c: (0, 0)),
            pl.BlockSpec(right.shape, lambda c: (0, 0)),
            pl.BlockSpec((1, next_), lambda c: (0, 0)),
            pl.BlockSpec((chunk, ext_rows, next_), lambda c: (c, 0, 0)),
        ],
        out_specs=pl.BlockSpec((chunk, ext_rows, next_), lambda c: (c, 0, 0)),
        out_shape=jax.ShapeDtypeStruct(amplitudes.shape, BF16),
        scratch_shapes=[
            pltpu.VMEM((pairs, nblk, WIDTH), F32),
            pltpu.VMEM((ext_rows, 1), F32),
        ],
        compiler_params=pltpu.CompilerParams(
            dimension_semantics=("arbitrary",),
            vmem_limit_bytes=min(60, nblk) * 1024 * 1024,
        ),
        name="residual",
    )(raws, left, right, energies[None], held)


def solution(mesh):
    return jax.shard_map(
        shards,
        mesh=mesh,
        in_specs=(
            P("pb", "sp", None),
            P(),
            P(),
            P("sp", None),
            P("sp", None),
            P("sp"),
            P(),
            P("pb", None),
        ),
        out_specs=P("pb", "sp", None),
        check_vma=False,
    )
```

time: 169 us -> 51.8 us (0.31)
  blocking collectives: 117 us -> 37.7 us
  local copies, waits for them, and re-layouts: 30.2 us -> 0.01 us
  matrix products: 18.6 us -> 0 us
  Pallas kernels: 0 us -> 13.2 us
    psum x1 -> x0, blocking collectives: 80.3 us -> none  [shards(): lax.psum(term.reshape(nblk, pairs, width), 'sp').astype(jnp.bfloat16)]
    all_to_all x0 -> x3, blocking collectives: none -> 37.7 us  [the longest x1 16.1 us: shards(): lax.all_to_all(partial.reshape(n * halves, pairs, LANES), ('sp', 'pb'), 0...]
    all_gather x1 -> x0, blocking collectives: 36.9 us -> none  [shards(): every = lax.all_gather(raw[None], ('sp', 'pb'), axis=0, tiled=True)]
    dot_general x5 -> x0, matrix products: 18.6 us -> none  [the longest x1 7.57 us: shards(): jnp.einsum('pab,nb->pan', amplitudes, virtuals, preferred_element_type=jn...]
    pallas_call x0 -> x4, Pallas kernels: none -> 13.2 us  [the longest x1 6.65 us: shards(): pl.pallas_call(functools.partial(back_kernel, nblk, chunk), in_specs=[HBM...]
    convert_element_type x2 -> x0, local copies, waits for them, and re-layouts: 11.4 us -> none  [the longest x1 10.8 us: shards(): half = jnp.einsum('pab,nb->pan', amplitudes, virtuals, preferred_element_...]
    gather x4 -> x0, local copies, waits for them, and re-layouts: 8.88 us -> none  [the longest x1 5.49 us: shards(): right = half[:, :, highs[:, None] + col_span[None, :]]]
    reshape x4 -> x0, local copies, waits for them, and re-layouts: 6.21 us -> none  [the longest x2 4.85 us: shards(): term.reshape(nblk, pairs, width)]
where the time goes in v3:
time: 51.8 us; the launch traced here: 51.5 us
  blocking collectives  37.7 us (73%)
  Pallas kernels  13.2 us (25%)
  between operations  0.69 us (1%)
    all_to_all x1, blocking collectives, shards(): lax.all_to_all(partial.reshape(n * halves, pairs, LANES), ('sp', 'pb'), 0...  16.1 us
    all_to_all x1, blocking collectives, shards(): ao_all = lax.all_to_all(ao, 'sp', 0, 0, tiled=True)  11.2 us
    all_to_all x1, blocking collectives, shards(): raws = lax.all_to_all(raw, 'sp', 0, 0, tiled=True)  10.3 us
    pallas_call x1, Pallas kernels, shards(): pl.pallas_call(functools.partial(back_kernel, nblk, chunk), in_specs=[HBM...  6.65 us
    pallas_call x1, Pallas kernels, shards(): pl.pallas_call(functools.partial(residual_kernel, nblk, ext_rows), grid=(...  5.83 us

profile of v3, /device:TPU:0, one launch (start us, length us, event | category | flops | bytes accessed | tf_op | source)
XLA Modules:
  0.0 51.5 jit_solution(4315982021887016993)
XLA Ops:
  0.7 0.0 copy-start
  0.7 0.0 copy-start.1
  0.7 6.6 %back.1 = (bf16[16,2,20,128]{3,2,1,0:T(8,128)(2,1)S(1)}, bf16[256,1024]{1,0:T(8,128)(2,1)S(1)}, bf16[128,64]{1,0:T(8,128)(2,1)S(1)}, bf16[20,64,1024]{2,1,0:T(8,...) custom-call(s32[2,16]{1,0:T(2,128)} %offs_in.1, s32[1,16]{1,0:T(1,128)} %lists_in.1, ...), custom_call_target="tpu_custom_call" | custom-call | tf_op jit(solution)/shard_map/back/pallas_call | solution.py:258
  7.3 16.1 %all_to_all.15.got = bf16[32,20,128]{2,1,0:T(8,128)(2,1)S(1)} all-to-all(bf16[32,20,128]{2,1,0:T(8,128)(2,1)S(1)} %bitcast.2), channel_id=1, replica_groups=mesh['sp'=16,'pb'=2] {'sp','pb'}, dimensions={0} | all-to-all | bytes 327680 | tf_op jit(solution)/shard_map/all_to_all | solution.py:283
  23.4 0.0 copy-done
  23.4 0.2 mix.1
  23.6 11.2 %all_to_all.16.got = bf16[16,32,128]{2,1,0:T(8,128)(2,1)S(1)} all-to-all(bf16[16,32,128]{2,1,0:T(8,128)(2,1)S(1)} %mix.1), channel_id=1, replica_groups=mesh['sp'=16,'pb'=2] {'sp'}, dimensions={0} | all-to-all | bytes 262144 | tf_op jit(solution)/shard_map/all_to_all | solution.py:295
  34.8 0.5 %raw.1 = bf16[16,20,128]{2,1,0:T(8,128)(2,1)S(1)} custom-call(bf16[256,256]{1,0:T(8,128)(2,1)S(1)} %get-tuple-element.11.pick, bf16[16,32,128]{2,1,0:T(8,128)(2,1)S(1)} %all_to_all.16.got, bf16[128,2048]{1,0:T(8,128)(2,1)S(1)} %get-tuple-element.13.slab), custom_call_target="tpu_custom_call" | custom-call | tf_op jit(solution)/shard_map/raw/pallas_call | solution.py:296
  35.4 10.3 %all_to_all.17.raws = bf16[16,20,128]{2,1,0:T(8,128)(2,1)S(1)} all-to-all(bf16[16,20,128]{2,1,0:T(8,128)(2,1)S(1)} %raw.1), channel_id=1, replica_groups=mesh['sp'=16,'pb'=2] {'sp'}, dimensions={0} | all-to-all | bytes 163840 | tf_op jit(solution)/shard_map/all_to_all | solution.py:305
  45.7 0.0 copy-done.1
  45.7 5.8 %residual.1 = bf16[20,64,1024]{2,1,0:T(8,128)(2,1)} custom-call(bf16[16,20,128]{2,1,0:T(8,128)(2,1)S(1)} %all_to_all.17.raws, bf16[128,64]{1,0:T(8,128)(2,1)S(1)} %get-tuple-element.14.left, bf16[256,1024]{1,0:T(8,128)(2,1)S(1)} %get-tuple-element.15.right, f32[1,1024]{1,0:T(1,128)S(1)} %bitcast.3, bf16[20,64,1024]{2,1,0:T(8,128)(2,1)S(1)} %get-tuple-element.16.amp), custom_call_target="tpu_custom_call" | custom-call | tf_op jit(solution)/shard_map/residual/pallas_call | solution.py:306
Async XLA Ops:
  0.7 22.8 %copy-start = (bf16[20,40]{1,0:T(8,128)(2,1)S(1)}, bf16[20,40]{1,0:T(8,128)(2,1)}, u32[]{:S(2)}) copy-start(bf16[20,40]{1,0:T(8,128)(2,1)} %coupling.1) | copy-start | bytes 4804
  0.7 45.0 %copy-start.1 = (f32[1024]{0:T(1024)S(1)}, f32[1024]{0:T(1024)}, u32[]{:S(2)}) copy-start(f32[1024]{0:T(1024)} %param.10) | copy-start | bytes 12292

commit v4 on v3

v4 whole, which is shorter than its diff:
```python
import functools

import jax
import jax.numpy as jnp
from jax import lax
from jax.experimental import pallas as pl
from jax.experimental.pallas import tpu as pltpu
from jax.sharding import PartitionSpec as P

SHELL_ROW = 8
SHELL_COL = 16
WIDTH = SHELL_ROW * SHELL_COL
SUB = 16
RIGHT_WIN = 32
LEFT_WIN = 16
LANES = 128
PACK = 32
F32 = jnp.float32
BF16 = jnp.bfloat16
VMEM = pl.BlockSpec(memory_space=pltpu.VMEM)
SMEM = pl.BlockSpec(memory_space=pltpu.SMEM)
HBM = pl.BlockSpec(memory_space=pltpu.HBM)


def iota(shape, dim):
    return lax.broadcasted_iota(jnp.int32, shape, dim)


def dot(a, b):
    return jnp.dot(a, b, preferred_element_type=F32)


def dot_t(a, b):
    return lax.dot_general(a, b, (((1,), (1,)), ((), ())), preferred_element_type=F32)


def chunk_of(pairs):
    return max(c for c in range(1, 6) if pairs % c == 0)


def window(low, size, nao):
    base = jnp.minimum(low // 8 * 8, nao - size)
    return pl.multiple_of(base, 8)


def picks(offs, which, first, count, shell, size, nao):
    cols = count * size
    row, col = iota((shell, cols), 0), iota((shell, cols), 1)
    parts = []
    for t in range(count):
        low = offs[which, first + t]
        delta = low - window(low, size, nao) + t * size
        parts.append(jnp.where(col == row + delta, 1.0, 0.0))
    return jnp.concatenate(parts, axis=0).astype(BF16)


def back_kernel(
    nblk, offs_in, lists_in, live, amp, virt, slab,
    out, right, left_wide, amps, slab_out, pick_out,
    offs, lists, right_win, left_win, left, acc, sems, amp_sems,
):
    pairs, ext_rows, next_ = amp.shape
    nao = virt.shape[0]
    slots = lists.shape[1]
    whole, cols = nblk * SHELL_COL, slots * SHELL_COL
    first = lax.axis_index("sp") * ext_rows
    lane_base = pl.multiple_of(first // LANES * LANES, LANES)
    shift = first - lane_base
    facts = [
        pltpu.make_async_copy(offs_in, offs, amp_sems.at[0]),
        pltpu.make_async_copy(lists_in, lists, amp_sems.at[1]),
    ]
    for fact in facts:
        fact.start()
    amp_load = pltpu.make_async_copy(amp, amps, amp_sems.at[2])
    amp_load.start()
    facts[0].wait()
    rights, lefts = [], []
    for b in range(nblk):
        base = window(offs[1, b], RIGHT_WIN, nao)
        rights.append(
            pltpu.make_async_copy(
                virt.at[pl.ds(base, RIGHT_WIN), :], right_win.at[b], sems.at[0, b]
            )
        )
        rights[-1].start()
    for b in range(nblk):
        base = window(offs[0, b], LEFT_WIN, nao)
        lefts.append(
            pltpu.make_async_copy(
                virt.at[pl.ds(base, LEFT_WIN), pl.ds(lane_base, LANES)],
                left_win.at[b],
                sems.at[1, b],
            )
        )
        lefts[-1].start()
    slab_load = pltpu.make_async_copy(slab, slab_out, amp_sems.at[3])
    slab_load.start()

    half_sub = SUB // 2
    right_picks = [
        picks(offs, 1, g * half_sub, half_sub, SHELL_COL, RIGHT_WIN, nao)
        for g in range(nblk // half_sub)
    ]
    left_picks = [
        picks(offs, 0, g * SUB, SUB, SHELL_ROW, LEFT_WIN, nao) for g in range(nblk // SUB)
    ]
    lane_pick = jnp.where(
        iota((LANES, ext_rows), 0) == iota((LANES, ext_rows), 1) + shift, 1.0, 0.0
    ).astype(BF16)
    high, span = SUB * SHELL_ROW, SUB * SHELL_COL
    facts[1].wait()
    lane = iota((1, cols), 1)
    target = jnp.full((1, cols), -1, jnp.int32)
    for k in range(slots):
        block = jnp.where(k < live[0], lists[0, k], -whole)
        target = jnp.where(
            lane // SHELL_COL == k, block * SHELL_COL + lane % SHELL_COL, target
        )
    pick_out[...] = jnp.where(iota((whole, cols), 0) == target, 1.0, 0.0).astype(BF16)

    for load in rights:
        load.wait()
    rows, depth = half_sub * SHELL_COL, half_sub * RIGHT_WIN
    for g, pick in enumerate(right_picks):
        win = right_win[g * half_sub : (g + 1) * half_sub].reshape(depth, next_)
        right[g * rows : (g + 1) * rows, :] = dot(pick, win).astype(BF16)
    for load in lefts:
        load.wait()
    for g, pick in enumerate(left_picks):
        win = left_win[g * SUB : (g + 1) * SUB].reshape(SUB * LEFT_WIN, LANES)
        wide = dot(pick, win).astype(BF16)
        part = dot(wide, lane_pick).astype(BF16)
        left[g * high : (g + 1) * high, :] = part
        down, across = iota((high, span), 0), iota((high, span), 1)
        for i in range(SHELL_ROW):
            place = (down // SHELL_ROW == across // SHELL_COL) & (down % SHELL_ROW == i)
            left_wide[i, :, g * span : (g + 1) * span] = lax.dot_general(
                part,
                jnp.where(place, 1.0, 0.0).astype(BF16),
                (((0,), (0,)), ((), ())),
                preferred_element_type=F32,
            )

    block_of = iota((SHELL_ROW, span), 1) // SHELL_COL
    amp_load.wait()
    half = dot_t(amps[...].reshape(pairs * ext_rows, next_), right[...]).astype(BF16)
    for q in range(pairs):
        own = half[q * ext_rows : (q + 1) * ext_rows]
        for g in range(nblk // SUB):
            full = dot(left[g * high : (g + 1) * high, :], own[:, g * span : (g + 1) * span])
            kept = full[:SHELL_ROW]
            for t in range(1, SUB):
                kept = jnp.where(
                    block_of == t, full[t * SHELL_ROW : (t + 1) * SHELL_ROW], kept
                )
            acc[:, q, g * span : (g + 1) * span] = kept
    tiles = whole // LANES
    for i in range(SHELL_ROW):
        for t in range(tiles):
            done = acc[i, :, t * LANES : (t + 1) * LANES].astype(BF16)
            for h in range(out.shape[1]):
                out[i * tiles + t, h] = done
    slab_load.wait()


def mix_kernel(n, halves, got, coupling, out):
    pairs = coupling.shape[0]
    sums = []
    for h in range(halves):
        total = got[h].astype(F32)
        for s in range(1, n):
            total = total + got[s * halves + h].astype(F32)
        sums.append(total)
    ao = jnp.concatenate(sums, axis=0).astype(BF16)
    mixed = dot(coupling[...], ao).astype(BF16)
    for d in range(n):
        out[d, :pairs] = mixed
        out[d, pairs:] = jnp.zeros((out.shape[1] - pairs, LANES), BF16)


def raw_kernel(pairs, pick, got, slab, out):
    n, rows, _ = got.shape
    tiles = n // SHELL_ROW
    cols = pick.shape[1]
    slots = cols // SHELL_COL
    held = got[...].reshape(SHELL_ROW, tiles, rows, LANES)
    ao = jnp.concatenate(
        [held[:, t].reshape(SHELL_ROW * rows, LANES) for t in range(tiles)], axis=1
    )
    chosen = dot(ao, pick[...])
    need = -(-pairs // 8) * 8
    per = LANES // SHELL_COL
    group = iota((need, LANES), 1) // SHELL_COL
    turned = {}
    for i in range(SHELL_ROW):
        for t in range(cols // LANES):
            tile = chosen[i * rows : i * rows + need, t * LANES : (t + 1) * LANES]
            for m in range(per):
                turned[i, t, m] = pltpu.roll(tile, m * SHELL_COL, 1) if m else tile
    laid = []
    for k in range(slots):
        t, at = k // per, k % per
        piece = turned[0, t, (0 - at) % per]
        for i in range(1, SHELL_ROW):
            piece = jnp.where(group == i, turned[i, t, (i - at) % per], piece)
        laid.append(piece)
    raw = dot_t(jnp.concatenate(laid, axis=1).astype(BF16), slab[...])
    done = raw[:pairs].astype(BF16)
    for d in range(n):
        out[d] = done


def residual_kernel(nblk, chunk, raws, left_wide, right, energies, amp, out, mixed, result, sems):
    n, pairs, _ = raws.shape
    ext_rows, next_ = amp.shape[1:]
    first = lax.axis_index("sp") * ext_rows
    lane_base = pl.multiple_of(first // LANES * LANES, LANES)
    near = energies[:, pl.ds(lane_base, LANES)]
    pick = iota((ext_rows, LANES), 1) == iota((ext_rows, LANES), 0) + (first - lane_base)
    own_e = jnp.sum(jnp.where(pick, near, 0.0), axis=1, keepdims=True)
    per = LANES // SHELL_COL
    group = iota((pairs, LANES), 1) // SHELL_COL
    for t in range(nblk // per):
        tiles = [raws[t * per + m].astype(F32) for m in range(per)]
        turned = {}
        for m in range(per):
            for turn in range(per):
                turned[m, turn] = pltpu.roll(tiles[m], turn * SHELL_COL, 1) if turn else tiles[m]
        for i in range(SHELL_ROW):
            piece = turned[0, (0 - i) % per]
            for m in range(1, per):
                piece = jnp.where(group == m, turned[m, (m - i) % per], piece)
            mixed[i, :, t * LANES : (t + 1) * LANES] = piece

    diag = own_e + energies[...]
    copies = []
    for c in range(pairs // chunk):
        uppers = []
        for q in range(c * chunk, (c + 1) * chunk):
            upper = left_wide[0] * mixed[0, q : q + 1, :]
            for i in range(1, SHELL_ROW):
                upper = upper + left_wide[i] * mixed[i, q : q + 1, :]
            uppers.append(upper.astype(BF16))
        part = pl.ds(c * chunk, chunk)
        inner = dot(jnp.concatenate(uppers, axis=0), right[...]).reshape(chunk, ext_rows, next_)
        result[part] = (inner + diag[None] * amp[part].astype(F32)).astype(BF16)
        copies.append(pltpu.make_async_copy(result.at[part], out.at[part], sems.at[c]))
        copies[-1].start()
    for copy in copies:
        copy.wait()


def shards(amplitudes, virtuals, energies, integrals, screened, counts, offsets, coupling):
    pairs, ext_rows, next_ = amplitudes.shape
    nblk = offsets.shape[1]
    n = lax.axis_size("sp")
    halves = lax.axis_size("pb")
    slots = screened.shape[1]
    span = nblk * SHELL_COL
    chunk = chunk_of(pairs)
    padded = -(-pairs // PACK) * PACK
    plain = pltpu.CompilerParams(vmem_limit_bytes=min(60, nblk) * 1024 * 1024)
    in_hbm = functools.partial(
        pltpu.with_memory_space_constraint, memory_space=pltpu.HBM
    )

    partial, right, left_wide, held, slab, pick = pl.pallas_call(
        functools.partial(back_kernel, nblk),
        in_specs=[HBM, HBM, SMEM, HBM, HBM, HBM],
        out_specs=[VMEM] * 6,
        out_shape=[
            jax.ShapeDtypeStruct((n, halves, pairs, LANES), BF16),
            jax.ShapeDtypeStruct((span, next_), BF16),
            jax.ShapeDtypeStruct((SHELL_ROW, ext_rows, span), F32),
            jax.ShapeDtypeStruct(amplitudes.shape, BF16),
            jax.ShapeDtypeStruct(integrals.shape, BF16),
            jax.ShapeDtypeStruct((span, slots * SHELL_COL), BF16),
        ],
        scratch_shapes=[
            pltpu.SMEM(offsets.shape, jnp.int32),
            pltpu.SMEM(screened.shape, jnp.int32),
            pltpu.VMEM((nblk, RIGHT_WIN, next_), BF16),
            pltpu.VMEM((nblk, LEFT_WIN, LANES), BF16),
            pltpu.VMEM((nblk * SHELL_ROW, ext_rows), BF16),
            pltpu.VMEM((SHELL_ROW, pairs, span), F32),
            pltpu.SemaphoreType.DMA((2, nblk)),
            pltpu.SemaphoreType.DMA((4,)),
        ],
        compiler_params=plain,
        name="back",
    )(
        in_hbm(offsets),
        in_hbm(screened),
        counts,
        in_hbm(amplitudes),
        in_hbm(virtuals),
        in_hbm(integrals),
    )

    got = lax.all_to_all(
        partial.reshape(n * halves, pairs, LANES), ("sp", "pb"), 0, 0, tiled=True
    )
    ao = pl.pallas_call(
        functools.partial(mix_kernel, n, halves),
        in_specs=[VMEM, VMEM],
        out_specs=VMEM,
        out_shape=jax.ShapeDtypeStruct((n, padded, LANES), BF16),
        compiler_params=plain,
        name="mix",
    )(got, coupling)

    ao_all = lax.all_to_all(ao, "sp", 0, 0, tiled=True)
    raw = pl.pallas_call(
        functools.partial(raw_kernel, pairs),
        in_specs=[VMEM] * 3,
        out_specs=VMEM,
        out_shape=jax.ShapeDtypeStruct((n, pairs, WIDTH), BF16),
        compiler_params=plain,
        name="raw",
    )(pick, ao_all, slab)

    raws = lax.all_to_all(raw, "sp", 0, 0, tiled=True)
    return pl.pallas_call(
        functools.partial(residual_kernel, nblk, chunk),
        in_specs=[VMEM] * 5,
        out_specs=HBM,
        out_shape=jax.ShapeDtypeStruct(amplitudes.shape, BF16),
        scratch_shapes=[
            pltpu.VMEM((SHELL_ROW, pairs, span), F32),
            pltpu.VMEM(amplitudes.shape, BF16),
            pltpu.SemaphoreType.DMA((pairs // chunk,)),
        ],
        compiler_params=plain,
        name="residual",
    )(raws, left_wide, right, energies[None], held)


def solution(mesh):
    return jax.shard_map(
        shards,
        mesh=mesh,
        in_specs=(
            P("pb", "sp", None),
            P(),
            P(),
            P("sp", None),
            P("sp", None),
            P("sp"),
            P(),
            P("pb", None),
        ),
        out_specs=P("pb", "sp", None),
        check_vma=False,
    )
```

time: 51.8 us -> 47.2 us (0.911)
  Pallas kernels: 13.2 us -> 8.61 us
    pallas_call x2, Pallas kernels: 12.5 us -> 7.9 us  [the longest x1 5.05 us: shards(): pl.pallas_call(functools.partial(back_kernel, nblk), in_specs=[HBM, HBM,...]
where the time goes in v4:
time: 47.2 us; the launch traced here: 47 us
  blocking collectives  37.7 us (80%)
  Pallas kernels  8.61 us (18%)
  between operations  0.69 us (1%)
    all_to_all x1, blocking collectives, shards(): lax.all_to_all(partial.reshape(n * halves, pairs, LANES), ('sp', 'pb'), 0...  16.1 us
    all_to_all x1, blocking collectives, shards(): ao_all = lax.all_to_all(ao, 'sp', 0, 0, tiled=True)  11.2 us
    all_to_all x1, blocking collectives, shards(): raws = lax.all_to_all(raw, 'sp', 0, 0, tiled=True)  10.3 us
    pallas_call x1, Pallas kernels, shards(): pl.pallas_call(functools.partial(back_kernel, nblk), in_specs=[HBM, HBM,...  5.05 us
    pallas_call x1, Pallas kernels, shards(): pl.pallas_call(functools.partial(residual_kernel, nblk, chunk), in_specs=...  2.85 us

profile of v4, /device:TPU:0, one launch (start us, length us, event | category | flops | bytes accessed | tf_op | source)
XLA Modules:
  0.0 47.0 jit_solution(12207288245634436150)
XLA Ops:
  0.7 0.0 copy-start
  0.7 0.0 copy-start.1
  0.7 5.1 %back.1 = (bf16[16,2,20,128]{3,2,1,0:T(8,128)(2,1)S(1)}, bf16[256,1024]{1,0:T(8,128)(2,1)S(1)}, f32[8,64,256]{2,1,0:T(8,128)S(1)}, bf16[20,64,1024]{2,1,0:T(8,12...) custom-call(s32[2,16]{1,0:T(2,128)} %offs_in.1, s32[1,16]{1,0:T(1,128)} %lists_in.1, ...), custom_call_target="tpu_custom_call" | custom-call | tf_op jit(solution)/shard_map/back/pallas_call | solution.py:268
  5.7 16.1 %all_to_all.15.got = bf16[32,20,128]{2,1,0:T(8,128)(2,1)S(1)} all-to-all(bf16[32,20,128]{2,1,0:T(8,128)(2,1)S(1)} %bitcast.2), channel_id=1, replica_groups=mesh['sp'=16,'pb'=2] {'sp','pb'}, dimensions={0} | all-to-all | bytes 327680 | tf_op jit(solution)/shard_map/all_to_all | solution.py:301
  21.8 0.0 copy-done
  21.8 0.2 mix.1
  22.0 11.2 %all_to_all.16.got = bf16[16,32,128]{2,1,0:T(8,128)(2,1)S(1)} all-to-all(bf16[16,32,128]{2,1,0:T(8,128)(2,1)S(1)} %mix.1), channel_id=1, replica_groups=mesh['sp'=16,'pb'=2] {'sp'}, dimensions={0} | all-to-all | bytes 262144 | tf_op jit(solution)/shard_map/all_to_all | solution.py:313
  33.2 0.5 %raw.1 = bf16[16,20,128]{2,1,0:T(8,128)(2,1)S(1)} custom-call(bf16[256,256]{1,0:T(8,128)(2,1)S(1)} %get-tuple-element.11.pick, bf16[16,32,128]{2,1,0:T(8,128)(2,1)S(1)} %all_to_all.16.got, bf16[128,2048]{1,0:T(8,128)(2,1)S(1)} %get-tuple-element.13.slab), custom_call_target="tpu_custom_call" | custom-call | tf_op jit(solution)/shard_map/raw/pallas_call | solution.py:314
  33.8 10.3 %all_to_all.17.raws = bf16[16,20,128]{2,1,0:T(8,128)(2,1)S(1)} all-to-all(bf16[16,20,128]{2,1,0:T(8,128)(2,1)S(1)} %raw.1), channel_id=1, replica_groups=mesh['sp'=16,'pb'=2] {'sp'}, dimensions={0} | all-to-all | bytes 163840 | tf_op jit(solution)/shard_map/all_to_all | solution.py:323
  44.1 0.0 copy-done.1
  44.1 2.9 %residual.1 = bf16[20,64,1024]{2,1,0:T(8,128)(2,1)} custom-call(bf16[16,20,128]{2,1,0:T(8,128)(2,1)S(1)} %all_to_all.17.raws, f32[8,64,256]{2,1,0:T(8,128)S(1)} %get-tuple-element.14.left_wide, bf16[256,1024]{1,0:T(8,128)(2,1)S(1)} %get-tuple-element.15.right, f32[1,1024]{1,0:T(1,128)S(1)} %bitcast.3, bf16[20,64,1024]{2,1,0:T(8,128)(2,1)S(1)} %get-tuple-element.16.amp), custom_call_target="tpu_custom_call" | custom-call | tf_op jit(solution)/shard_map/residual/pallas_call | solution.py:324
Async XLA Ops:
  0.7 21.2 %copy-start = (bf16[20,40]{1,0:T(8,128)(2,1)S(1)}, bf16[20,40]{1,0:T(8,128)(2,1)}, u32[]{:S(2)}) copy-start(bf16[20,40]{1,0:T(8,128)(2,1)} %coupling.1) | copy-start | bytes 4804
  0.7 43.5 %copy-start.1 = (f32[1024]{0:T(1024)S(1)}, f32[1024]{0:T(1024)}, u32[]{:S(2)}) copy-start(f32[1024]{0:T(1024)} %param.10) | copy-start | bytes 12292
